TPU v7x, 512 devices: a whole 4x8x8 slice. The times are simulated.
512 devices in a mesh: req: 64 (over z_lo, x, y), tp: 8 (over z_hi, core).
Axes of the slice: x: 4, y: 8, z: 8 (z_hi: 4, z_lo: 2; z = z_hi * 2 + z_lo), core: 2. Of those that a mesh axis runs over, the one named last changes fastest.
Arguments:
- q_proj: bfloat16 [64, 128, 3072], P('req', None, 'tp'), may hold values from -24 to 24, as said below
- kv_proj: bfloat16 [64, 128, 2, 1024], P('req', None, None, 'tp'), may hold values from -6 to 6
- q_bias: bfloat16 [3072], P('tp'), may hold values from -3 to 3
- kv_bias: bfloat16 [2, 1024], P(None, 'tp'), may hold values from -3 to 3
- prefix_kv: bfloat16 [64, 1024, 2, 1024], P('req', None, None, 'tp'), may hold values from -24 to 24, as said below
- lengths: int32 [64], P('req'), may hold values from 1 to 128, 4096 in all
- group_of: int32 [64], P('req'), may hold values from 0 to 2
- owner: int32 [3], replicated, may hold values from 0 to 63
- positions: int32 [64, 128], P('req'), may hold values from 1024 to 1278, as said below
- residual: bfloat16 [64, 128, 5120], P('req', None, 'tp'), may hold values from -6 to 6
- out_weight: bfloat16 [3072, 5120], P(None, 'tp'), may hold values from -0.109375 to 0.109375
Outputs:
- hidden: bfloat16 [64, 128, 5120], P('req', None, 'tp')
Inputs may be any that keep to these rules, and one draw needn't show every extreme that they name: `q_proj`: projected queries; entries stay within the stated bounds. `prefix_kv`: cached keys are already rotated at prefix positions 0 to 1023. Each request's positions are a start of 1024 or more plus the slot index.
All inputs are finite; a program needn't handle non-finite values. No bound on the sum of `lengths` on one device may be relied on, other than what follows from the above.
Results may differ from a plain program's by a relative error of at most 0.006.
Values may be sent and summed in bfloat16 or wider, within the bound.
No kernel may reach another device: no remote copies, remote signals or barrier semaphores. Data moves between devices by JAX's collectives and lax.ppermute only.
A program may use at most 128 MiB of HBM per device.

v0:
```python
import math
import jax
import jax.numpy as jnp
from jax import lax
from jax.sharding import PartitionSpec as P

HD = 128


def spread(x, axis, root):
    mine = lax.axis_index(axis) == root
    return lax.psum(jnp.where(mine, x, jnp.zeros_like(x)), axis)


def rotate(vectors, places):
    half = HD // 2
    index = jnp.arange(half).astype(jnp.float32)
    freqs = jnp.exp(index * (-2.0 / HD) * math.log(1000000.0))
    angles = places.astype(jnp.float32)[:, None] * freqs[None, :]
    cosine = jnp.concatenate([jnp.cos(angles), jnp.cos(angles)], axis=-1)[:, None, :]
    sine = jnp.concatenate([jnp.sin(angles), jnp.sin(angles)], axis=-1)[:, None, :]
    turned = jnp.concatenate([-vectors[..., half:], vectors[..., :half]], axis=-1)
    return vectors * cosine + turned * sine


def attend_rows(queries, all_keys, all_vals, length, prefix_len):
    count = queries.shape[0]
    slots = jnp.arange(count)
    causal = slots[None, :] <= slots[:, None]
    allowed = jnp.concatenate([jnp.ones((count, prefix_len), dtype=bool), causal], axis=1)
    scores = jnp.einsum("rhd,kd->hrk", queries, all_keys, preferred_element_type=jnp.float32) * (
        1.0 / math.sqrt(HD)
    )
    scores = jnp.where(allowed[None], scores, -1e30)
    top = jnp.max(scores, axis=-1, keepdims=True)
    weights = jnp.where(allowed[None], jnp.exp(scores - top), 0.0)
    total = jnp.sum(weights, axis=-1)
    rounded = weights.astype(jnp.bfloat16)
    mixed = jnp.einsum("hrk,kd->rhd", rounded, all_vals, preferred_element_type=jnp.float32)
    mixed = mixed / jnp.transpose(total)[:, :, None]
    mixed = jnp.where((slots < length)[:, None, None], mixed, 0.0)
    return mixed.astype(jnp.bfloat16)


def body(
    q_proj,
    kv_proj,
    q_bias,
    kv_bias,
    prefix_kv,
    lengths,
    group_of,
    owner,
    positions,
    residual,
    out_weight,
):
    cap = q_proj.shape[1]
    prefix_len = prefix_kv.shape[1]
    mine = group_of[0]
    length = lengths[0]
    places = positions[0]
    queries = q_proj[0].astype(jnp.float32).reshape(cap, -1, HD) + q_bias.astype(
        jnp.float32
    ).reshape(-1, HD)
    queries = rotate(queries, places).astype(jnp.bfloat16)
    pairs = kv_proj[0].astype(jnp.float32) + kv_bias.astype(jnp.float32)
    keys = rotate(pairs[:, 0][:, None, :], places)[:, 0].astype(jnp.bfloat16)
    vals = pairs[:, 1].astype(jnp.bfloat16)
    slab = jnp.zeros_like(prefix_kv[0])
    for group in range(owner.shape[0]):
        received = spread(prefix_kv[0], "req", owner[group])
        slab = jnp.where(mine == group, received, slab)
    all_keys = jnp.concatenate([slab[:, 0], keys], axis=0)
    all_vals = jnp.concatenate([slab[:, 1], vals], axis=0)
    attended = attend_rows(queries, all_keys, all_vals, length, prefix_len)
    attended = attended.reshape(cap, -1)
    whole_heads = lax.all_gather(attended, "tp", axis=1, tiled=True)
    projected = jnp.dot(whole_heads, out_weight, preferred_element_type=jnp.float32)
    hidden = (residual[0].astype(jnp.float32) + projected).astype(jnp.bfloat16)
    return hidden[None]


def solution(mesh):
    in_specs = (
        P("req", None, "tp"),
        P("req", None, None, "tp"),
        P("tp"),
        P(None, "tp"),
        P("req", None, None, "tp"),
        P("req"),
        P("req"),
        P(),
        P("req", None),
        P("req", None, "tp"),
        P(None, "tp"),
    )
    out_specs = P("req", None, "tp")
    return jax.shard_map(body, mesh=mesh, in_specs=in_specs, out_specs=out_specs, check_vma=False)
```

profile of v0, /device:TPU:1, one launch (start us, length us, event | category | flops | bytes accessed | tf_op | source)
XLA Modules:
  0.0 664.5 jit_solution(9709575429134257465)
XLA Ops:
  6.5 0.0 all-reduce.4.cloned.1.call-start
  6.5 1.4 fusion.31
  9.9 0.0 copy-start.4
  9.9 0.0 copy-start.1
  9.9 2.3 select_bitcast_fusion
  12.2 0.0 copy-start.5
  12.2 0.0 copy-start.2
  12.2 0.0 copy-start.3
  12.2 0.0 all-reduce.4.cloned.1.call-update
  12.9 0.0 copy-done.4
  12.9 0.3 fusion.22
  13.3 0.1 pad_maximum_fusion
  13.4 0.1 copy.24
  13.5 0.1 copy.25
  13.6 0.0 copy-done.1
  13.6 0.1 copy.23
  13.7 0.0 copy-done.5
  14.4 0.0 copy-done.2
  14.5 0.0 copy-done.3
  14.5 0.1 slice_negate_fusion.1
  14.6 0.1 fusion.21
  14.7 0.1 convert_add_fusion
  14.9 0.1 fusion.17
  15.0 570.6 %all-reduce.4.cloned.1.call-done = (bf16[1024,2,128]{2,0,1:T(8,128)(2,1)}, bf16[1024,2,128]{2,0,1:T(8,128)(2,1)}, bf16[1024,2,128]{2,0,1:T(8,128)(2,1)}) async-done(((bf16[1024,2,128]{2,0,1:T(8,128)(2,1)}, bf16[1024,2,128]{2,0,1:T(8,128)(2,1)}, bf16[1024,2,128]{2,0,1:T(8,128)(2,1)}), (bf16[1024,2,128]{2,0,1:T(8,128)(2,1)}, bf16[1024,2,128]{2,0,1:T(8,128)(2,1)}, ...) | async-done | bytes 1572880 | tf_op jit(solution)/shard_map/psum | solution.py:12
  585.6 1.1 select_select_fusion
  586.7 0.9 fusion.32
  587.7 0.4 fusion.3
  588.1 0.0 copy-start
  588.1 0.6 fusion.10
  588.7 65.4 %all_gather.3 = bf16[128,3072]{0,1:T(8,128)(2,1)S(1)} all-gather(bf16[128,384]{0,1:T(8,128)(2,1)S(1)} %bitcast.78), channel_id=1, replica_groups=mesh['req'=64,'tp'=8] {'tp'}, dimensions={1}, use_global_device_ids=true | all-gather | bytes 884736 | tf_op jit(solution)/shard_map/all_gather | solution.py:78
  654.0 0.0 copy-done
  654.0 3.6 fusion.9
  (11 shorter events, 0.2 us)
Async XLA Ops:
  6.5 579.0 %all-reduce.4.cloned.1.call-start = ((), (), s32[]{:S(2)}) async-start(), calls=%async_computation | async-start | bytes 3145728 | tf_op jit(solution)/shard_map/psum | solution.py:12
  9.9 3.1 copy-start.4
  9.9 3.7 copy-start.1
  12.2 1.5 copy-start.5
  12.2 2.2 copy-start.2
  12.2 2.3 copy-start.3
  588.1 65.9 %copy-start = (bf16[1,128,640]{2,1,0:T(8,128)(2,1)S(1)}, bf16[1,128,640]{2,1,0:T(8,128)(2,1)}, u32[]{:S(2)}) copy-start(bf16[1,128,640]{2,1,0:T(8,128)(2,1)} %param.20) | copy-start | bytes 491524
Sparse Core Ops, SparseCore 0:
  12.4 573.1 all-reduce.3
where the time goes:
time: 665 us; the launch traced here: 664 us
  waiting for transfers between devices  571 us (86%)
  blocking collectives  65.4 us (10%)
  between operations  16.8 us (3%)
    psum x1, waiting for transfers between devices, spread(): return lax.psum(jnp.where(mine, x, jnp.zeros_like(x)), axis)  571 us
    all_gather x1, blocking collectives, body(): whole_heads = lax.all_gather(attended, 'tp', axis=1, tiled=True)  65.4 us
  transfers between devices with their start and end apart: 1, of which 1 were waited for; matrix products, arithmetic and copies ran while one was open for 0% of the time, Pallas kernels for 0%

commit v1 on v0

--- a/solution.py
+++ b/solution.py
@@ -5,11 +5,12 @@
 from jax.sharding import PartitionSpec as P
 
 HD = 128
+start_widths = lambda local, comm_axis: jnp.sum(lax.all_gather(local, axis_name=comm_axis), axis=0)
 
 
 def spread(x, axis, root):
     mine = lax.axis_index(axis) == root
-    return lax.psum(jnp.where(mine, x, jnp.zeros_like(x)), axis)
+    return start_widths(jnp.where(mine, x, jnp.zeros_like(x)), axis)
 
 
 def rotate(vectors, places):

time: 665 us -> 1200 us (1.80)
  waiting for transfers between devices: 571 us -> 1110 us
  blocking collectives: 65.4 us -> 26 us
  other arithmetic: 4.34 us -> 37.3 us
    all_gather x0 -> x3, waiting for transfers between devices: none -> 1110 us  [lax.all_gather(local, axis_name=comm_axis)]
    psum x1 -> x0, waiting for transfers between devices: 571 us -> none  [spread(): return lax.psum(jnp.where(mine, x, jnp.zeros_like(x)), axis)]
    all_gather x1, blocking collectives: 65.4 us -> 26 us  [body(): whole_heads = lax.all_gather(attended, 'tp', axis=1, tiled=True)]
    reduce_sum x0 -> x3, other arithmetic: none -> 34.1 us  [jnp.sum(lax.all_gather(local, axis_name=comm_axis), axis=0)]
  transfers between devices with their start and end apart: 1 -> 3, of which waited for: 1 -> 3; matrix products, arithmetic and copies ran while one was open for 0% -> 2% of each run, Pallas kernels for 0% -> 0%
where the time goes in v1:
time: 1200 us
  waiting for transfers between devices  1110 us (92%)
  other arithmetic  37.3 us (3%)
  blocking collectives  26 us (2%)
  between operations  16.5 us (1%)
    all_gather x3, waiting for transfers between devices, lax.all_gather(local, axis_name=comm_axis)  1110 us
    reduce_sum x3, other arithmetic, jnp.sum(lax.all_gather(local, axis_name=comm_axis), axis=0)  34.1 us
    all_gather x1, blocking collectives, body(): whole_heads = lax.all_gather(attended, 'tp', axis=1, tiled=True)  26 us
  transfers between devices with their start and end apart: 3, of which 3 were waited for; matrix products, arithmetic and copies ran while one was open for 2% of the time, Pallas kernels for 0%

profile of v1, /device:TPU:1, one launch (start us, length us, event | category | flops | bytes accessed | tf_op | source)
XLA Modules:
  0.0 1197.5 jit_solution(7919726225042141972)
XLA Ops:
  6.5 1.4 fusion.31
  9.7 0.0 copy-start.4
  9.7 0.0 copy-start.1
  9.8 2.3 broadcast_select_fusion
  12.0 0.0 all-gather.4.cloned.1.call-update
  12.1 0.0 all-gather.6.cloned.1.call-start
  12.1 0.7 all-gather.6.cloned.1.call-update
  12.8 0.0 all-gather.8.cloned.1.call-start
  12.9 0.7 all-gather.8.cloned.1.call-update
  14.2 0.3 fusion.22
  14.5 0.1 pad_maximum_fusion
  14.7 0.1 copy.34
  14.7 0.1 copy.35
  14.9 0.0 copy-done.1
  14.9 0.1 copy.33
  15.8 0.1 slice_negate_fusion.1
  15.9 0.1 fusion.21
  16.0 0.1 convert_add_fusion
  16.2 0.1 fusion.17
  16.3 375.7 %all-gather.4.cloned.1.call-done = bf16[64,1024,2,128]{3,1,2,0:T(8,128)(2,1)} async-done(((bf16[1,1024,2,128]{3,1,2,0:T(8,128)(2,1)}), bf16[64,1024,2,128]{3,1,2,0:T(8,128)(2,1)}) %all-gather.4.cloned.1.call-update) | async-done | bytes 33554448 | tf_op jit(solution)/shard_map/all_gather | solution.py:8
  392.0 11.4 reduce_sum.45
  403.4 366.3 %all-gather.6.cloned.1.call-done = bf16[64,1024,2,128]{3,1,2,0:T(8,128)(2,1)} async-done(((bf16[1,1024,2,128]{3,1,2,0:T(8,128)(2,1)}), bf16[64,1024,2,128]{3,1,2,0:T(8,128)(2,1)}) %all-gather.6.cloned.1.call-update) | async-done | bytes 33554448 | tf_op jit(solution)/shard_map/all_gather | solution.py:8
  769.7 11.4 reduce_sum.46
  781.1 366.9 %all-gather.8.cloned.1.call-done = bf16[64,1024,2,128]{3,1,2,0:T(8,128)(2,1)} async-done(((bf16[1,1024,2,128]{3,1,2,0:T(8,128)(2,1)}), bf16[64,1024,2,128]{3,1,2,0:T(8,128)(2,1)}) %all-gather.8.cloned.1.call-update) | async-done | bytes 33554448 | tf_op jit(solution)/shard_map/all_gather | solution.py:8
  1147.9 11.4 reduce_sum.47
  1159.3 0.1 select_select_fusion
  1159.4 0.9 fusion.32
  1160.3 0.4 fusion.3
  1160.8 0.0 copy-start
  1160.8 0.6 fusion.10
  1161.3 26.0 %all_gather.18 = bf16[128,3072]{0,1:T(8,128)(2,1)S(1)} all-gather(bf16[128,384]{0,1:T(8,128)(2,1)S(1)} %bitcast.72), channel_id=1, replica_groups=mesh['req'=64,'tp'=8] {'tp'}, dimensions={1}, use_global_device_ids=true | all-gather | bytes 884736 | tf_op jit(solution)/shard_map/all_gather | solution.py:79
  1187.3 3.6 fusion.9
  (20 shorter events, 0.2 us)
Async XLA Ops:
  6.5 385.5 %all-gather.4.cloned.1.call-start = ((), (), s32[]{:S(2)}) async-start(), calls=%async_computation | async-start | bytes 34078720 | tf_op jit(solution)/shard_map/all_gather | solution.py:8
  9.7 4.5 copy-start.4
  9.7 5.1 copy-start.1
  12.0 3.0 copy-start.5
  12.0 3.7 copy-start.3
  12.0 3.7 copy-start.2
  12.1 757.6 %all-gather.6.cloned.1.call-start = ((), (), s32[]{:S(2)}) async-start(), calls=%async_computation.1 | async-start | bytes 34078720 | tf_op jit(solution)/shard_map/all_gather | solution.py:8
  12.8 1135.1 %all-gather.8.cloned.1.call-start = ((), (), s32[]{:S(2)}) async-start(), calls=%async_computation.2 | async-start | bytes 34078720 | tf_op jit(solution)/shard_map/all_gather | solution.py:8
  1160.8 26.6 %copy-start = (bf16[1,128,640]{2,1,0:T(8,128)(2,1)S(1)}, bf16[1,128,640]{2,1,0:T(8,128)(2,1)}, u32[]{:S(2)}) copy-start(bf16[1,128,640]{2,1,0:T(8,128)(2,1)} %param.20) | copy-start | bytes 491524
Sparse Core Ops, SparseCore 0:
  12.2 379.7 all-gather.3
  394.1 375.5 all-gather.5
  771.8 376.0 all-gather.7
